TPU v7x, 256 devices: a whole 4x4x8 slice. The times are simulated.
256 devices in a mesh: ctx: 32 (over z, y_lo, core), head: 8 (over x, y_hi).
Axes of the slice: x: 4, y: 4 (y_hi: 2, y_lo: 2; y = y_hi * 2 + y_lo), z: 8, core: 2. Of those that a mesh axis runs over, the one named last changes fastest.
Arguments:
- query: bfloat16 [4096, 8192], P('ctx', 'head'), may hold values from -11 to 11
- key_in: bfloat16 [4096, 1024], P('ctx', 'head'), may hold values from -11 to 11
- value: bfloat16 [4096, 1024], P('ctx', 'head'), may hold values from -6 to 6
- grad_y: bfloat16 [4096, 8192], P('ctx', 'head'), may hold values from -6 to 6
- w_out: bfloat16 [8192, 8192], P('head', 'ctx'), may hold values from -0.0625 to 0.0625
- parent: int32 [32], replicated, may hold values from 1 to 31, as said below
Outputs:
- grad_query: bfloat16 [4096, 8192], P('ctx', 'head')
- grad_key: bfloat16 [4096, 1024], P('ctx', 'head')
- grad_value: bfloat16 [4096, 1024], P('ctx', 'head')
Inputs may be any that keep to these rules, and one draw needn't show every extreme that they name: The shared prefix is blocks 32 - 4 to 31: parent[31] = 31 and parent[b] = b + 1 for the other prefix blocks; the earlier blocks form particles of 4 consecutive blocks, in which each block's parent is the block after it, except a particle's last block, whose parent is a block of the shared prefix.
All inputs are finite; a program needn't handle non-finite values.
Results may differ from a plain program's by a relative error of at most 0.014.
Values may be sent and summed in bfloat16 or wider, within the bound.
A program may use at most 128 MiB of HBM per device.

v0:
```python
import jax
import jax.numpy as jnp
from jax import lax
from jax.sharding import PartitionSpec as P

HPG = 8
DH = 128
BLOCK = 128


def shifted(value, axis, steps):
    count = lax.axis_size(axis)
    pairs = [(source, (source + steps) % count) for source in range(count)]
    return lax.ppermute(value, axis, pairs)


def ancestors(parent):
    count = parent.shape[0]
    index = jnp.arange(count, dtype=jnp.int32)
    start = (index[:, None] == index[None, :]).astype(jnp.int32)

    def advance(step, state):
        current, marks = state
        current = jnp.sum(jnp.where(current[:, None] == index[None, :], parent[None, :], 0), axis=1)
        marks = jnp.maximum(marks, (current[:, None] == index[None, :]).astype(jnp.int32))
        return (current, marks)

    return lax.fori_loop(0, count, advance, (index, start))[1]


def per_device(query, key_in, value, grad_y, w_out, parent):
    tokens_here = query.shape[0]
    groups = key_in.shape[1] // DH
    scale = DH ** (-0.5)
    cycle_size = lax.axis_size("ctx")
    place = lax.axis_index("ctx")
    full_rows = lax.all_gather(grad_y, "head", axis=1, tiled=True)
    grad_attn = lax.dot_general(
        full_rows,
        lax.all_gather(w_out, "ctx", axis=1, tiled=True),
        (((1,), (1,)), ((), ())),
        preferred_element_type=jnp.float32,
    ).astype(jnp.bfloat16)
    visible = ancestors(parent)
    block_count = parent.shape[0]
    blocks_here = tokens_here // BLOCK
    local_visible = lax.dynamic_slice_in_dim(visible, place * blocks_here, blocks_here, 0).astype(
        jnp.float32
    )
    query_pos = place * tokens_here + jnp.arange(tokens_here, dtype=jnp.int32)
    query_block = query_pos // BLOCK
    owned = place * blocks_here + jnp.arange(blocks_here, dtype=jnp.int32)
    query_select = (query_block[:, None] == owned[None, :]).astype(jnp.float32)
    query_visible = jnp.dot(query_select, local_visible)
    block_index = jnp.arange(block_count, dtype=jnp.int32)

    def make_mask(start, count):
        key_pos = start + jnp.arange(count, dtype=jnp.int32)
        key_block = key_pos // BLOCK
        key_select = (key_block[:, None] == block_index[None, :]).astype(jnp.float32)
        allowed = jnp.dot(query_visible, key_select.T) > 0.5
        return allowed & (
            (query_block[:, None] != key_block[None, :]) | (key_pos[None, :] <= query_pos[:, None])
        )

    query_heads = query.reshape(tokens_here, groups, HPG, DH).transpose(1, 2, 0, 3)
    grad_heads = grad_attn.reshape(tokens_here, groups, HPG, DH).transpose(1, 2, 0, 3)

    def split_heads(matrix):
        return matrix.reshape(matrix.shape[0], groups, DH).transpose(1, 0, 2)

    def join_heads(tensor):
        return tensor.transpose(1, 0, 2).reshape(tensor.shape[1], groups * DH)

    stat_shape = (groups, HPG, tokens_here)
    key_piece = lax.all_gather(key_in, "ctx", axis=0, tiled=True)
    value_piece = lax.all_gather(value, "ctx", axis=0, tiled=True)
    mask = make_mask(jnp.int32(0), key_piece.shape[0])
    statistics_top = jnp.full(stat_shape, -1e30, jnp.float32)
    scores = (
        jnp.einsum(
            "ghqd,gkd->ghqk",
            query_heads,
            split_heads(key_piece),
            preferred_element_type=jnp.float32,
        )
        * scale
    )
    masked = jnp.where(mask, scores, -1e30)
    new_top = jnp.maximum(statistics_top, jnp.max(masked, axis=3))
    weights = jnp.where(mask, jnp.exp(scores - new_top[..., None]), 0.0)
    dprob = jnp.einsum(
        "ghqd,gkd->ghqk", grad_heads, split_heads(value_piece), preferred_element_type=jnp.float32
    )
    statistics_norm = jnp.sum(weights, axis=3)
    weighted = jnp.sum(weights * dprob, axis=3)
    top, norm, weighted = (new_top, statistics_norm, weighted)
    delta = weighted / norm

    def contribution(key_piece, value_piece, mask):
        key_heads = split_heads(key_piece)
        value_heads = split_heads(value_piece)
        scores = (
            jnp.einsum("ghqd,gkd->ghqk", query_heads, key_heads, preferred_element_type=jnp.float32)
            * scale
        )
        prob = jnp.where(mask, jnp.exp(scores - top[..., None]), 0.0) / norm[..., None]
        dprob = jnp.einsum(
            "ghqd,gkd->ghqk", grad_heads, value_heads, preferred_element_type=jnp.float32
        )
        value_part = jnp.einsum(
            "ghqk,ghqd->gkd",
            prob.astype(jnp.bfloat16),
            grad_heads,
            preferred_element_type=jnp.float32,
        )
        dscore = (prob * (dprob - delta[..., None])).astype(jnp.bfloat16)
        query_part = (
            jnp.einsum("ghqk,gkd->ghqd", dscore, key_heads, preferred_element_type=jnp.float32)
            * scale
        )
        key_part = (
            jnp.einsum("ghqk,ghqd->gkd", dscore, query_heads, preferred_element_type=jnp.float32)
            * scale
        )
        return (query_part, join_heads(key_part), join_heads(value_part))

    def visit(key_piece, value_piece, start):
        mask = make_mask(start, key_piece.shape[0])
        return contribution(key_piece, value_piece, mask)

    grad_query = jnp.zeros((groups, HPG, tokens_here, DH), jnp.float32)

    def turn_one(step, state):
        grad_q, key_piece, value_piece, key_sum, value_sum = state
        owner = (place - step) % cycle_size
        query_part, key_part, value_part = visit(key_piece, value_piece, owner * tokens_here)
        grad_q = grad_q + query_part
        key_sum = key_sum + key_part
        value_sum = value_sum + value_part
        key_piece, value_piece = shifted((key_piece, value_piece), "ctx", 1)
        key_sum, value_sum = shifted((key_sum, value_sum), "ctx", 1)
        return (grad_q, key_piece, value_piece, key_sum, value_sum)

    zero_rows = jnp.zeros((tokens_here, groups * DH), jnp.float32)
    state = (grad_query, key_in, value, zero_rows, zero_rows)
    grad_query, unused_key, unused_value, grad_key, grad_value = lax.fori_loop(
        0, cycle_size, turn_one, state
    )
    grad_query = (
        grad_query.transpose(2, 0, 1, 3)
        .reshape(tokens_here, groups * HPG * DH)
        .astype(jnp.bfloat16)
    )
    return (grad_query, grad_key.astype(jnp.bfloat16), grad_value.astype(jnp.bfloat16))


def solution(mesh):
    placed = (
        P("ctx", "head"),
        P("ctx", "head"),
        P("ctx", "head"),
        P("ctx", "head"),
        P("head", "ctx"),
        P(),
    )
    return jax.shard_map(
        per_device,
        mesh=mesh,
        in_specs=placed,
        out_specs=(P("ctx", "head"), P("ctx", "head"), P("ctx", "head")),
        check_vma=False,
    )
```

profile of v0, /device:TPU:2, one launch (start us, length us, event | category | flops | bytes accessed | tf_op | source)
XLA Modules:
  0.0 608.8 jit_solution(9453911751109003068)
XLA Ops:
  12.1 29.5 %while.40 = (s32[]{:T(128)}, s32[32]{0:T(128)S(1)}, s32[32,32]{1,0:T(8,128)S(1)}, s32[32]{0:T(128)}, s32[]{:T(128)}) while((s32[]{:T(128)}, s32[32]{0:T(128)S(1)}, s32[32,32]{1,0:T(8,128)S(1)}, s32[32]{0:T(128)}, s32[]{:T(128)}) %tuple.80), condition=%wide.region_2.3_spmd.clone.clone, body=%wide.region_0.2_spmd.clone.clone.sunk | while | flops 6114 | bytes 9021 | solution.py:28
  43.7 33.4 %all-gather.5.cloned.1.call-done = bf16[4096,128]{1,0:T(8,128)(2,1)} async-done(((bf16[128,128]{1,0:T(8,128)(2,1)}), bf16[4096,128]{1,0:T(8,128)(2,1)}) %all-gather.5.cloned.1.call-update) | async-done | bytes 1048592 | tf_op jit(solution)/shard_map/all_gather | solution.py:76
  77.2 4.5 select_reduce_fusion.1
  81.7 5.7 copy-done
  87.4 4.9 fusion.35
  92.3 47.1 %all-gather.7.cloned.1.call-done = bf16[128,8192]{1,0:T(8,128)(2,1)} async-done(((bf16[128,1024]{1,0:T(8,128)(2,1)}), bf16[128,8192]{1,0:T(8,128)(2,1)}) %all-gather.7.cloned.1.call-update) | async-done | bytes 2097168 | tf_op jit(solution)/shard_map/all_gather | solution.py:37
  139.3 123.7 %all-gather.9.cloned.1.call-done = bf16[1024,8192]{1,0:T(8,128)(2,1)} async-done(((bf16[1024,256]{1,0:T(8,128)(2,1)}), bf16[1024,8192]{1,0:T(8,128)(2,1)}) %all-gather.9.cloned.1.call-update) | async-done | bytes 16777232 | tf_op jit(solution)/shard_map/all_gather | solution.py:40
  263.0 12.1 %fusion.38 = bf16[16,8,8,128]{3,1,2,0:T(8,128)(2,1)S(1)} fusion(bf16[128,8192]{1,0:T(8,128)(2,1)} %all-gather.7.cloned.1.call-done, bf16[1024,8192]{1,0:T(8,128)(2,1)} %all-gather.9.cloned.1.call-done), kind=kOutput, calls=%fused_computation.60 | convolution fusion | flops 2147614720 | bytes 19136512 | tf_op jit(solution)/shard_map/dot_general | solution.py:38
  275.2 52.8 %all-gather.11.cloned.1.call-done = bf16[4096,128]{1,0:T(8,128)(2,1)} async-done(((bf16[128,128]{1,0:T(8,128)(2,1)}), bf16[4096,128]{1,0:T(8,128)(2,1)}) %all-gather.11.cloned.1.call-update) | async-done | bytes 1048592 | tf_op jit(solution)/shard_map/all_gather | solution.py:77
  328.1 9.0 %multiply_reduce_fusion = f32[8,128]{1,0:T(8,128)S(1)} fusion(f32[8,128,4096]{2,1,0:T(8,128)} %copy-done, f32[8,128]{1,0:T(8,128)S(1)} %get-tuple-element.648, pred[128,4096]{1,0:T(8,128)(4,1)S(1)} %fusion.36, bf16[4096,128]{1,0:T(8,128)(2,1)} %all-gather.11.cloned.1.call-done, bf16[128,1,8,128]{3,2,0,1:T(8,128)(2,1)S(1)} %bitcast.121), kind=kOutput, calls=%fused_computation.51 | convolution fusion | flops 1094712320 | bytes 18620416 | tf_op jit(solution)/shard_map/ghqd,gkd->ghqk/dot_general | solution.py:92
  337.1 263.0 %while.41 = (s32[]{:T(128)}, f32[1,8,128,128]{3,2,1,0:T(8,128)S(1)}, bf16[128,128]{1,0:T(8,128)(2,1)S(1)}, bf16[128,128]{1,0:T(8,128)(2,1)S(1)}, f32[128,128]{1,...) while((s32[]{:T(128)}, ...), condition=%wide.region_7.8_spmd.clone.clone.clone, body=%wide.region_6.7_spmd.clone.clone.clone.sunk | while | flops 170405904 | bytes 5817452 | solution.py:147
  343.2 2.5 collective-permute-done.2
  360.3 1.7 collective-permute-done.2
  364.7 1.8 collective-permute-start.3
  373.7 2.6 collective-permute-done.1
  381.8 2.7 collective-permute-done.1
  390.5 2.2 collective-permute-done.1
  397.4 2.5 collective-permute-start.3
  405.8 2.2 collective-permute-start.3
  409.4 1.9 collective-permute-done.2
  414.0 2.2 collective-permute-start.3
  417.8 1.7 collective-permute-done.2
  422.2 2.2 collective-permute-start.3
  426.0 1.7 collective-permute-done.2
  430.4 2.2 collective-permute-start.3
  438.6 2.2 collective-permute-start.3
  442.3 1.7 collective-permute-done.2
  446.7 2.2 collective-permute-start.3
  454.9 2.2 collective-permute-start.3
  458.7 1.7 collective-permute-done.2
  463.1 2.2 collective-permute-start.3
  471.3 2.2 collective-permute-start.3
  475.0 1.7 collective-permute-done.2
  479.4 2.2 collective-permute-start.3
  487.6 2.2 collective-permute-start.3
  495.8 2.2 collective-permute-start.3
  504.0 2.2 collective-permute-start.3
  512.2 2.2 collective-permute-start.3
  520.3 2.2 collective-permute-start.3
  528.5 2.2 collective-permute-start.3
  536.7 2.2 collective-permute-start.3
  544.9 2.2 collective-permute-start.3
  553.0 2.2 collective-permute-start.3
  561.2 2.2 collective-permute-start.3
  569.4 2.2 collective-permute-start.3
  577.6 2.2 collective-permute-start.3
  585.7 2.2 collective-permute-start.3
  593.9 2.2 collective-permute-start.3
  (703 shorter events, 219.4 us)
Async XLA Ops:
  7.2 70.0 %all-gather.5.cloned.1.call-start = ((), (), s32[]{:S(2)}) async-start(), calls=%async_computation | async-start | bytes 1081344 | tf_op jit(solution)/shard_map/all_gather | solution.py:76
  10.0 129.4 %all-gather.7.cloned.1.call-start = ((), (), s32[]{:S(2)}) async-start(), calls=%async_computation.1 | async-start | bytes 2359296 | tf_op jit(solution)/shard_map/all_gather | solution.py:37
  10.7 252.3 %all-gather.9.cloned.1.call-start = ((), (), s32[]{:S(2)}) async-start(), calls=%async_computation.2 | async-start | bytes 17301504 | tf_op jit(solution)/shard_map/all_gather | solution.py:40
  11.5 316.6 %all-gather.11.cloned.1.call-start = ((), (), s32[]{:S(2)}) async-start(), calls=%async_computation.3 | async-start | bytes 1081344 | tf_op jit(solution)/shard_map/all_gather | solution.py:77
  339.8 5.9 collective-permute-start.2
  340.4 6.0 collective-permute-start.3
  348.0 5.9 collective-permute-start.2
  348.3 6.2 %collective-permute-start.3 = (f32[128,128]{1,0:T(8,128)S(1)}, f32[128,128]{1,0:T(8,128)S(1)}, u32[]{:S(2)}, u32[]{:S(2)}) collective-permute-start(f32[128,128]{1,0:T(8,128)S(1)} %fusion.91), channel_id=1, source_target_pairs={{0,8},{8,16},{16,24},{24,32},{32,40},{40,48},{48,56},{56,64},{64,7... | collective-permute-start | bytes 196616 | tf_op jit(solution)/shard_map/while/body/eval_jaxpr/ppermute | solution.py:14
  356.1 5.9 collective-permute-start.2
  356.5 6.2 %collective-permute-start.3 = (f32[128,128]{1,0:T(8,128)S(1)}, f32[128,128]{1,0:T(8,128)S(1)}, u32[]{:S(2)}, u32[]{:S(2)}) collective-permute-start(f32[128,128]{1,0:T(8,128)S(1)} %fusion.91), channel_id=1, source_target_pairs={{0,8},{8,16},{16,24},{24,32},{32,40},{40,48},{48,56},{56,64},{64,7... | collective-permute-start | bytes 196616 | tf_op jit(solution)/shard_map/while/body/eval_jaxpr/ppermute | solution.py:14
  364.3 5.9 collective-permute-start.2
  364.7 6.2 %collective-permute-start.3 = (f32[128,128]{1,0:T(8,128)S(1)}, f32[128,128]{1,0:T(8,128)S(1)}, u32[]{:S(2)}, u32[]{:S(2)}) collective-permute-start(f32[128,128]{1,0:T(8,128)S(1)} %fusion.91), channel_id=1, source_target_pairs={{0,8},{8,16},{16,24},{24,32},{32,40},{40,48},{48,56},{56,64},{64,7... | collective-permute-start | bytes 196616 | tf_op jit(solution)/shard_map/while/body/eval_jaxpr/ppermute | solution.py:14
  372.5 5.9 collective-permute-start.2
  372.9 6.2 %collective-permute-start.3 = (f32[128,128]{1,0:T(8,128)S(1)}, f32[128,128]{1,0:T(8,128)S(1)}, u32[]{:S(2)}, u32[]{:S(2)}) collective-permute-start(f32[128,128]{1,0:T(8,128)S(1)} %fusion.91), channel_id=1, source_target_pairs={{0,8},{8,16},{16,24},{24,32},{32,40},{40,48},{48,56},{56,64},{64,7... | collective-permute-start | bytes 196616 | tf_op jit(solution)/shard_map/while/body/eval_jaxpr/ppermute | solution.py:14
  381.0 6.2 %collective-permute-start.3 = (f32[128,128]{1,0:T(8,128)S(1)}, f32[128,128]{1,0:T(8,128)S(1)}, u32[]{:S(2)}, u32[]{:S(2)}) collective-permute-start(f32[128,128]{1,0:T(8,128)S(1)} %fusion.91), channel_id=1, source_target_pairs={{0,8},{8,16},{16,24},{24,32},{32,40},{40,48},{48,56},{56,64},{64,7... | collective-permute-start | bytes 196616 | tf_op jit(solution)/shard_map/while/body/eval_jaxpr/ppermute | solution.py:14
  389.2 6.2 %collective-permute-start.3 = (f32[128,128]{1,0:T(8,128)S(1)}, f32[128,128]{1,0:T(8,128)S(1)}, u32[]{:S(2)}, u32[]{:S(2)}) collective-permute-start(f32[128,128]{1,0:T(8,128)S(1)} %fusion.91), channel_id=1, source_target_pairs={{0,8},{8,16},{16,24},{24,32},{32,40},{40,48},{48,56},{56,64},{64,7... | collective-permute-start | bytes 196616 | tf_op jit(solution)/shard_map/while/body/eval_jaxpr/ppermute | solution.py:14
  397.4 6.2 %collective-permute-start.3 = (f32[128,128]{1,0:T(8,128)S(1)}, f32[128,128]{1,0:T(8,128)S(1)}, u32[]{:S(2)}, u32[]{:S(2)}) collective-permute-start(f32[128,128]{1,0:T(8,128)S(1)} %fusion.91), channel_id=1, source_target_pairs={{0,8},{8,16},{16,24},{24,32},{32,40},{40,48},{48,56},{56,64},{64,7... | collective-permute-start | bytes 196616 | tf_op jit(solution)/shard_map/while/body/eval_jaxpr/ppermute | solution.py:14
  405.4 5.9 collective-permute-start.2
  405.8 6.1 %collective-permute-start.3 = (f32[128,128]{1,0:T(8,128)S(1)}, f32[128,128]{1,0:T(8,128)S(1)}, u32[]{:S(2)}, u32[]{:S(2)}) collective-permute-start(f32[128,128]{1,0:T(8,128)S(1)} %fusion.91), channel_id=1, source_target_pairs={{0,8},{8,16},{16,24},{24,32},{32,40},{40,48},{48,56},{56,64},{64,7... | collective-permute-start | bytes 196616 | tf_op jit(solution)/shard_map/while/body/eval_jaxpr/ppermute | solution.py:14
  413.6 5.9 collective-permute-start.2
  414.0 6.1 %collective-permute-start.3 = (f32[128,128]{1,0:T(8,128)S(1)}, f32[128,128]{1,0:T(8,128)S(1)}, u32[]{:S(2)}, u32[]{:S(2)}) collective-permute-start(f32[128,128]{1,0:T(8,128)S(1)} %fusion.91), channel_id=1, source_target_pairs={{0,8},{8,16},{16,24},{24,32},{32,40},{40,48},{48,56},{56,64},{64,7... | collective-permute-start | bytes 196616 | tf_op jit(solution)/shard_map/while/body/eval_jaxpr/ppermute | solution.py:14
  421.8 5.9 collective-permute-start.2
  422.2 6.1 %collective-permute-start.3 = (f32[128,128]{1,0:T(8,128)S(1)}, f32[128,128]{1,0:T(8,128)S(1)}, u32[]{:S(2)}, u32[]{:S(2)}) collective-permute-start(f32[128,128]{1,0:T(8,128)S(1)} %fusion.91), channel_id=1, source_target_pairs={{0,8},{8,16},{16,24},{24,32},{32,40},{40,48},{48,56},{56,64},{64,7... | collective-permute-start | bytes 196616 | tf_op jit(solution)/shard_map/while/body/eval_jaxpr/ppermute | solution.py:14
  429.9 5.9 collective-permute-start.2
  430.4 6.1 %collective-permute-start.3 = (f32[128,128]{1,0:T(8,128)S(1)}, f32[128,128]{1,0:T(8,128)S(1)}, u32[]{:S(2)}, u32[]{:S(2)}) collective-permute-start(f32[128,128]{1,0:T(8,128)S(1)} %fusion.91), channel_id=1, source_target_pairs={{0,8},{8,16},{16,24},{24,32},{32,40},{40,48},{48,56},{56,64},{64,7... | collective-permute-start | bytes 196616 | tf_op jit(solution)/shard_map/while/body/eval_jaxpr/ppermute | solution.py:14
  438.6 6.1 %collective-permute-start.3 = (f32[128,128]{1,0:T(8,128)S(1)}, f32[128,128]{1,0:T(8,128)S(1)}, u32[]{:S(2)}, u32[]{:S(2)}) collective-permute-start(f32[128,128]{1,0:T(8,128)S(1)} %fusion.91), channel_id=1, source_target_pairs={{0,8},{8,16},{16,24},{24,32},{32,40},{40,48},{48,56},{56,64},{64,7... | collective-permute-start | bytes 196616 | tf_op jit(solution)/shard_map/while/body/eval_jaxpr/ppermute | solution.py:14
  446.3 5.9 collective-permute-start.2
  446.7 6.1 %collective-permute-start.3 = (f32[128,128]{1,0:T(8,128)S(1)}, f32[128,128]{1,0:T(8,128)S(1)}, u32[]{:S(2)}, u32[]{:S(2)}) collective-permute-start(f32[128,128]{1,0:T(8,128)S(1)} %fusion.91), channel_id=1, source_target_pairs={{0,8},{8,16},{16,24},{24,32},{32,40},{40,48},{48,56},{56,64},{64,7... | collective-permute-start | bytes 196616 | tf_op jit(solution)/shard_map/while/body/eval_jaxpr/ppermute | solution.py:14
  454.5 5.9 collective-permute-start.2
  454.9 6.1 %collective-permute-start.3 = (f32[128,128]{1,0:T(8,128)S(1)}, f32[128,128]{1,0:T(8,128)S(1)}, u32[]{:S(2)}, u32[]{:S(2)}) collective-permute-start(f32[128,128]{1,0:T(8,128)S(1)} %fusion.91), channel_id=1, source_target_pairs={{0,8},{8,16},{16,24},{24,32},{32,40},{40,48},{48,56},{56,64},{64,7... | collective-permute-start | bytes 196616 | tf_op jit(solution)/shard_map/while/body/eval_jaxpr/ppermute | solution.py:14
  463.1 6.1 %collective-permute-start.3 = (f32[128,128]{1,0:T(8,128)S(1)}, f32[128,128]{1,0:T(8,128)S(1)}, u32[]{:S(2)}, u32[]{:S(2)}) collective-permute-start(f32[128,128]{1,0:T(8,128)S(1)} %fusion.91), channel_id=1, source_target_pairs={{0,8},{8,16},{16,24},{24,32},{32,40},{40,48},{48,56},{56,64},{64,7... | collective-permute-start | bytes 196616 | tf_op jit(solution)/shard_map/while/body/eval_jaxpr/ppermute | solution.py:14
  470.8 5.9 collective-permute-start.2
  471.3 6.1 %collective-permute-start.3 = (f32[128,128]{1,0:T(8,128)S(1)}, f32[128,128]{1,0:T(8,128)S(1)}, u32[]{:S(2)}, u32[]{:S(2)}) collective-permute-start(f32[128,128]{1,0:T(8,128)S(1)} %fusion.91), channel_id=1, source_target_pairs={{0,8},{8,16},{16,24},{24,32},{32,40},{40,48},{48,56},{56,64},{64,7... | collective-permute-start | bytes 196616 | tf_op jit(solution)/shard_map/while/body/eval_jaxpr/ppermute | solution.py:14
  479.4 6.1 %collective-permute-start.3 = (f32[128,128]{1,0:T(8,128)S(1)}, f32[128,128]{1,0:T(8,128)S(1)}, u32[]{:S(2)}, u32[]{:S(2)}) collective-permute-start(f32[128,128]{1,0:T(8,128)S(1)} %fusion.91), channel_id=1, source_target_pairs={{0,8},{8,16},{16,24},{24,32},{32,40},{40,48},{48,56},{56,64},{64,7... | collective-permute-start | bytes 196616 | tf_op jit(solution)/shard_map/while/body/eval_jaxpr/ppermute | solution.py:14
  487.6 6.1 %collective-permute-start.3 = (f32[128,128]{1,0:T(8,128)S(1)}, f32[128,128]{1,0:T(8,128)S(1)}, u32[]{:S(2)}, u32[]{:S(2)}) collective-permute-start(f32[128,128]{1,0:T(8,128)S(1)} %fusion.91), channel_id=1, source_target_pairs={{0,8},{8,16},{16,24},{24,32},{32,40},{40,48},{48,56},{56,64},{64,7... | collective-permute-start | bytes 196616 | tf_op jit(solution)/shard_map/while/body/eval_jaxpr/ppermute | solution.py:14
  495.8 6.1 %collective-permute-start.3 = (f32[128,128]{1,0:T(8,128)S(1)}, f32[128,128]{1,0:T(8,128)S(1)}, u32[]{:S(2)}, u32[]{:S(2)}) collective-permute-start(f32[128,128]{1,0:T(8,128)S(1)} %fusion.91), channel_id=1, source_target_pairs={{0,8},{8,16},{16,24},{24,32},{32,40},{40,48},{48,56},{56,64},{64,7... | collective-permute-start | bytes 196616 | tf_op jit(solution)/shard_map/while/body/eval_jaxpr/ppermute | solution.py:14
  504.0 6.1 %collective-permute-start.3 = (f32[128,128]{1,0:T(8,128)S(1)}, f32[128,128]{1,0:T(8,128)S(1)}, u32[]{:S(2)}, u32[]{:S(2)}) collective-permute-start(f32[128,128]{1,0:T(8,128)S(1)} %fusion.91), channel_id=1, source_target_pairs={{0,8},{8,16},{16,24},{24,32},{32,40},{40,48},{48,56},{56,64},{64,7... | collective-permute-start | bytes 196616 | tf_op jit(solution)/shard_map/while/body/eval_jaxpr/ppermute | solution.py:14
  512.2 6.1 %collective-permute-start.3 = (f32[128,128]{1,0:T(8,128)S(1)}, f32[128,128]{1,0:T(8,128)S(1)}, u32[]{:S(2)}, u32[]{:S(2)}) collective-permute-start(f32[128,128]{1,0:T(8,128)S(1)} %fusion.91), channel_id=1, source_target_pairs={{0,8},{8,16},{16,24},{24,32},{32,40},{40,48},{48,56},{56,64},{64,7... | collective-permute-start | bytes 196616 | tf_op jit(solution)/shard_map/while/body/eval_jaxpr/ppermute | solution.py:14
  520.3 6.1 %collective-permute-start.3 = (f32[128,128]{1,0:T(8,128)S(1)}, f32[128,128]{1,0:T(8,128)S(1)}, u32[]{:S(2)}, u32[]{:S(2)}) collective-permute-start(f32[128,128]{1,0:T(8,128)S(1)} %fusion.91), channel_id=1, source_target_pairs={{0,8},{8,16},{16,24},{24,32},{32,40},{40,48},{48,56},{56,64},{64,7... | collective-permute-start | bytes 196616 | tf_op jit(solution)/shard_map/while/body/eval_jaxpr/ppermute | solution.py:14
  528.5 6.1 %collective-permute-start.3 = (f32[128,128]{1,0:T(8,128)S(1)}, f32[128,128]{1,0:T(8,128)S(1)}, u32[]{:S(2)}, u32[]{:S(2)}) collective-permute-start(f32[128,128]{1,0:T(8,128)S(1)} %fusion.91), channel_id=1, source_target_pairs={{0,8},{8,16},{16,24},{24,32},{32,40},{40,48},{48,56},{56,64},{64,7... | collective-permute-start | bytes 196616 | tf_op jit(solution)/shard_map/while/body/eval_jaxpr/ppermute | solution.py:14
  536.7 6.1 %collective-permute-start.3 = (f32[128,128]{1,0:T(8,128)S(1)}, f32[128,128]{1,0:T(8,128)S(1)}, u32[]{:S(2)}, u32[]{:S(2)}) collective-permute-start(f32[128,128]{1,0:T(8,128)S(1)} %fusion.91), channel_id=1, source_target_pairs={{0,8},{8,16},{16,24},{24,32},{32,40},{40,48},{48,56},{56,64},{64,7... | collective-permute-start | bytes 196616 | tf_op jit(solution)/shard_map/while/body/eval_jaxpr/ppermute | solution.py:14
  544.9 6.1 %collective-permute-start.3 = (f32[128,128]{1,0:T(8,128)S(1)}, f32[128,128]{1,0:T(8,128)S(1)}, u32[]{:S(2)}, u32[]{:S(2)}) collective-permute-start(f32[128,128]{1,0:T(8,128)S(1)} %fusion.91), channel_id=1, source_target_pairs={{0,8},{8,16},{16,24},{24,32},{32,40},{40,48},{48,56},{56,64},{64,7... | collective-permute-start | bytes 196616 | tf_op jit(solution)/shard_map/while/body/eval_jaxpr/ppermute | solution.py:14
  553.0 6.1 %collective-permute-start.3 = (f32[128,128]{1,0:T(8,128)S(1)}, f32[128,128]{1,0:T(8,128)S(1)}, u32[]{:S(2)}, u32[]{:S(2)}) collective-permute-start(f32[128,128]{1,0:T(8,128)S(1)} %fusion.91), channel_id=1, source_target_pairs={{0,8},{8,16},{16,24},{24,32},{32,40},{40,48},{48,56},{56,64},{64,7... | collective-permute-start | bytes 196616 | tf_op jit(solution)/shard_map/while/body/eval_jaxpr/ppermute | solution.py:14
  561.2 6.1 %collective-permute-start.3 = (f32[128,128]{1,0:T(8,128)S(1)}, f32[128,128]{1,0:T(8,128)S(1)}, u32[]{:S(2)}, u32[]{:S(2)}) collective-permute-start(f32[128,128]{1,0:T(8,128)S(1)} %fusion.91), channel_id=1, source_target_pairs={{0,8},{8,16},{16,24},{24,32},{32,40},{40,48},{48,56},{56,64},{64,7... | collective-permute-start | bytes 196616 | tf_op jit(solution)/shard_map/while/body/eval_jaxpr/ppermute | solution.py:14
  569.4 6.1 %collective-permute-start.3 = (f32[128,128]{1,0:T(8,128)S(1)}, f32[128,128]{1,0:T(8,128)S(1)}, u32[]{:S(2)}, u32[]{:S(2)}) collective-permute-start(f32[128,128]{1,0:T(8,128)S(1)} %fusion.91), channel_id=1, source_target_pairs={{0,8},{8,16},{16,24},{24,32},{32,40},{40,48},{48,56},{56,64},{64,7... | collective-permute-start | bytes 196616 | tf_op jit(solution)/shard_map/while/body/eval_jaxpr/ppermute | solution.py:14
  577.6 6.1 %collective-permute-start.3 = (f32[128,128]{1,0:T(8,128)S(1)}, f32[128,128]{1,0:T(8,128)S(1)}, u32[]{:S(2)}, u32[]{:S(2)}) collective-permute-start(f32[128,128]{1,0:T(8,128)S(1)} %fusion.91), channel_id=1, source_target_pairs={{0,8},{8,16},{16,24},{24,32},{32,40},{40,48},{48,56},{56,64},{64,7... | collective-permute-start | bytes 196616 | tf_op jit(solution)/shard_map/while/body/eval_jaxpr/ppermute | solution.py:14
  585.7 6.1 %collective-permute-start.3 = (f32[128,128]{1,0:T(8,128)S(1)}, f32[128,128]{1,0:T(8,128)S(1)}, u32[]{:S(2)}, u32[]{:S(2)}) collective-permute-start(f32[128,128]{1,0:T(8,128)S(1)} %fusion.91), channel_id=1, source_target_pairs={{0,8},{8,16},{16,24},{24,32},{32,40},{40,48},{48,56},{56,64},{64,7... | collective-permute-start | bytes 196616 | tf_op jit(solution)/shard_map/while/body/eval_jaxpr/ppermute | solution.py:14
  593.9 6.1 %collective-permute-start.3 = (f32[128,128]{1,0:T(8,128)S(1)}, f32[128,128]{1,0:T(8,128)S(1)}, u32[]{:S(2)}, u32[]{:S(2)}) collective-permute-start(f32[128,128]{1,0:T(8,128)S(1)} %fusion.91), channel_id=1, source_target_pairs={{0,8},{8,16},{16,24},{24,32},{32,40},{40,48},{48,56},{56,64},{64,7... | collective-permute-start | bytes 196616 | tf_op jit(solution)/shard_map/while/body/eval_jaxpr/ppermute | solution.py:14
  (87 other events, 606.7 us)
Sparse Core Ops, SparseCore 0:
  10.4 66.7 all-gather.4
  79.8 59.4 all-gather.6
  141.1 121.8 all-gather.8
  265.3 62.7 all-gather.10
where the time goes:
time: 610 us; the launch traced here: 609 us
  waiting for transfers between devices  383 us (63%)
  matrix products  84.8 us (14%)
  starting transfers between devices  73.6 us (12%)
  other arithmetic  36.2 us (6%)
  local copies, waits for them, and re-layouts  14.8 us (2%)
  between operations  14 us (2%)
    all_gather x1, waiting for transfers between devices, per_device(): lax.all_gather(w_out, 'ctx', axis=1, tiled=True)  124 us
    ppermute x128, waiting for transfers between devices, shifted(): return lax.ppermute(value, axis, pairs)  124 us
    ppermute x128, starting transfers between devices, shifted(): return lax.ppermute(value, axis, pairs)  73.5 us
    all_gather x1, waiting for transfers between devices, per_device(): value_piece = lax.all_gather(value, 'ctx', axis=0, tiled=True)  52.8 us
    all_gather x1, waiting for transfers between devices, per_device(): full_rows = lax.all_gather(grad_y, 'head', axis=1, tiled=True)  47.1 us
    all_gather x1, waiting for transfers between devices, per_device(): key_piece = lax.all_gather(key_in, 'ctx', axis=0, tiled=True)  33.4 us
    reduce_sum x32, other arithmetic, advance(): jnp.sum(jnp.where(current[:, None] == index[None, :], parent[None, :], 0)...  26.9 us
    dot_general x32, matrix products, contribution(): jnp.einsum('ghqd,gkd->ghqk', query_heads, key_heads, preferred_element_ty...  17.2 us
  transfers between devices with their start and end apart: 132, of which 132 were waited for; matrix products, arithmetic and copies ran while one was open for 19% of the time, Pallas kernels for 0%

commit v1 on v0

--- a/solution.py
+++ b/solution.py
@@ -73,7 +73,9 @@
         return tensor.transpose(1, 0, 2).reshape(tensor.shape[1], groups * DH)
 
     stat_shape = (groups, HPG, tokens_here)
-    key_piece = lax.all_gather(key_in, "ctx", axis=0, tiled=True)
+    key_piece = jnp.concatenate(
+        lax.all_to_all(jnp.stack([key_in] * lax.axis_size("ctx")), "ctx", 0, 0), axis=0
+    )
     value_piece = lax.all_gather(value, "ctx", axis=0, tiled=True)
     mask = make_mask(jnp.int32(0), key_piece.shape[0])
     statistics_top = jnp.full(stat_shape, -1e30, jnp.float32)

time: 610 us -> 546 us (0.90)
  waiting for transfers between devices: 383 us -> 310 us
  starting transfers between devices: 73.6 us -> 83.4 us
    all_gather x1, waiting for transfers between devices: 47.1 us -> 7.81 us  [per_device(): full_rows = lax.all_gather(grad_y, 'head', axis=1, tiled=True)]
    all_gather x1 -> x0, waiting for transfers between devices: 33.4 us -> none  [per_device(): key_piece = lax.all_gather(key_in, 'ctx', axis=0, tiled=True)]
    all_to_all x0 -> x1, starting transfers between devices: none -> 9.87 us  [per_device(): lax.all_to_all(jnp.stack([key_in] * lax.axis_size('ctx')), 'ctx', 0, 0)]
  transfers between devices with their start and end apart: 132 -> 132, of which waited for: 132 -> 131; matrix products, arithmetic and copies ran while one was open for 19% -> 21% of each run, Pallas kernels for 0% -> 0%
where the time goes in v1:
time: 546 us; the launch traced here: 545 us
  waiting for transfers between devices  310 us (57%)
  matrix products  83.5 us (15%)
  starting transfers between devices  83.4 us (15%)
  other arithmetic  36.3 us (7%)
  local copies, waits for them, and re-layouts  15.4 us (3%)
  between operations  13.9 us (3%)
    all_gather x1, waiting for transfers between devices, per_device(): lax.all_gather(w_out, 'ctx', axis=1, tiled=True)  124 us
    ppermute x128, waiting for transfers between devices, shifted(): return lax.ppermute(value, axis, pairs)  124 us
    ppermute x128, starting transfers between devices, shifted(): return lax.ppermute(value, axis, pairs)  73.5 us
    all_gather x1, waiting for transfers between devices, per_device(): value_piece = lax.all_gather(value, 'ctx', axis=0, tiled=True)  53 us
    reduce_sum x32, other arithmetic, advance(): jnp.sum(jnp.where(current[:, None] == index[None, :], parent[None, :], 0)...  26.9 us
    dot_general x32, matrix products, contribution(): jnp.einsum('ghqd,gkd->ghqk', query_heads, key_heads, preferred_element_ty...  17.2 us
    dot_general x1, matrix products, per_device(): lax.dot_general(full_rows, lax.all_gather(w_out, 'ctx', axis=1, tiled=Tru...  12.1 us
  transfers between devices with their start and end apart: 132, of which 131 were waited for; matrix products, arithmetic and copies ran while one was open for 21% of the time, Pallas kernels for 0%

profile of v1, /device:TPU:2, one launch (start us, length us, event | category | flops | bytes accessed | tf_op | source)
XLA Modules:
  0.0 544.9 jit_solution(16485146466728743652)
XLA Ops:
  11.3 9.9 %all-to-all-start = ((bf16[32,128,128]{2,1,0:T(8,128)(2,1)}), bf16[32,128,128]{2,1,0:T(8,128)(2,1)S(1)}, u32[]{:S(2)}, u32[]{:S(2)}) async-start(bf16[32,128,128]{2,1,0:T(8,128)(2,1)} %stack.2), calls=%async_computation | async-start | bytes 2097152 | tf_op jit(solution)/shard_map/all_to_all | solution.py:77
  22.0 29.5 %while.40 = (s32[]{:T(128)}, s32[32]{0:T(128)S(1)}, s32[32,32]{1,0:T(8,128)S(1)}, s32[32]{0:T(128)}, s32[]{:T(128)}) while((s32[]{:T(128)}, s32[32]{0:T(128)S(1)}, s32[32,32]{1,0:T(8,128)S(1)}, s32[32]{0:T(128)}, s32[]{:T(128)}) %tuple.80), condition=%wide.region_2.3_spmd.clone.clone, body=%wide.region_0.2_spmd.clone.clone.sunk | while | flops 6114 | bytes 9021 | solution.py:28
  53.6 3.2 select_reduce_fusion.1
  56.8 5.7 %copy-done = f32[8,128,4096]{2,1,0:T(8,128)} copy-done((f32[8,128,4096]{2,1,0:T(8,128)}, f32[8,128,4096]{2,1,0:T(8,128)S(1)}, u32[]{:S(2)}) %copy-start) | copy-done | bytes 16777240
  62.5 4.9 fusion.35
  67.5 7.8 %all-gather.4.cloned.1.call-done = bf16[128,8192]{1,0:T(8,128)(2,1)} async-done(((bf16[128,1024]{1,0:T(8,128)(2,1)}), bf16[128,8192]{1,0:T(8,128)(2,1)}) %all-gather.4.cloned.1.call-update) | async-done | bytes 2097168 | tf_op jit(solution)/shard_map/all_gather | solution.py:37
  75.3 123.7 %all-gather.6.cloned.1.call-done = bf16[1024,8192]{1,0:T(8,128)(2,1)} async-done(((bf16[1024,256]{1,0:T(8,128)(2,1)}), bf16[1024,8192]{1,0:T(8,128)(2,1)}) %all-gather.6.cloned.1.call-update) | async-done | bytes 16777232 | tf_op jit(solution)/shard_map/all_gather | solution.py:40
  199.0 12.1 %fusion.38 = bf16[16,8,8,128]{3,1,2,0:T(8,128)(2,1)S(1)} fusion(bf16[128,8192]{1,0:T(8,128)(2,1)} %all-gather.4.cloned.1.call-done, bf16[1024,8192]{1,0:T(8,128)(2,1)} %all-gather.6.cloned.1.call-done), kind=kOutput, calls=%fused_computation.60 | convolution fusion | flops 2147614720 | bytes 19136512 | tf_op jit(solution)/shard_map/dot_general | solution.py:38
  211.2 53.0 %all-gather.8.cloned.1.call-done = bf16[4096,128]{1,0:T(8,128)(2,1)} async-done(((bf16[128,128]{1,0:T(8,128)(2,1)}), bf16[4096,128]{1,0:T(8,128)(2,1)}) %all-gather.8.cloned.1.call-update) | async-done | bytes 1048592 | tf_op jit(solution)/shard_map/all_gather | solution.py:79
  264.2 9.0 %multiply_reduce_fusion = f32[8,128]{1,0:T(8,128)S(1)} fusion(f32[8,128,4096]{2,1,0:T(8,128)} %copy-done, f32[8,128]{1,0:T(8,128)S(1)} %get-tuple-element.648, pred[128,4096]{1,0:T(8,128)(4,1)S(1)} %fusion.36, bf16[4096,128]{1,0:T(8,128)(2,1)} %all-gather.8.cloned.1.call-done, bf16[128,1,8,128]{3,2,0,1:T(8,128)(2,1)S(1)} %bitcast.121), kind=kOutput, calls=%fused_computation.51 | convolution fusion | flops 1094712320 | bytes 18620416 | tf_op jit(solution)/shard_map/ghqd,gkd->ghqk/dot_general | solution.py:94
  273.2 263.0 %while.41 = (s32[]{:T(128)}, f32[1,8,128,128]{3,2,1,0:T(8,128)S(1)}, bf16[128,128]{1,0:T(8,128)(2,1)S(1)}, bf16[128,128]{1,0:T(8,128)(2,1)S(1)}, f32[128,128]{1,...) while((s32[]{:T(128)}, ...), condition=%wide.region_7.8_spmd.clone.clone.clone, body=%wide.region_6.7_spmd.clone.clone.clone.sunk | while | flops 170405904 | bytes 5817452 | solution.py:149
  279.3 2.5 collective-permute-done.2
  300.8 1.8 collective-permute-start.3
  309.9 2.6 collective-permute-done.1
  318.0 2.7 collective-permute-done.1
  326.7 2.2 collective-permute-done.1
  333.5 2.5 collective-permute-start.3
  342.0 2.2 collective-permute-start.3
  345.6 1.9 collective-permute-done.2
  350.2 2.2 collective-permute-start.3
  353.9 1.7 collective-permute-done.2
  358.3 2.2 collective-permute-start.3
  362.1 1.7 collective-permute-done.2
  366.5 2.2 collective-permute-start.3
  374.7 2.2 collective-permute-start.3
  378.5 1.7 collective-permute-done.2
  382.9 2.2 collective-permute-start.3
  391.0 2.2 collective-permute-start.3
  394.8 1.7 collective-permute-done.2
  399.2 2.2 collective-permute-start.3
  407.4 2.2 collective-permute-start.3
  411.2 1.7 collective-permute-done.2
  415.6 2.2 collective-permute-start.3
  423.8 2.2 collective-permute-start.3
  427.5 1.7 collective-permute-done.2
  431.9 2.2 collective-permute-start.3
  440.1 2.2 collective-permute-start.3
  448.3 2.2 collective-permute-start.3
  456.5 2.2 collective-permute-start.3
  464.6 2.2 collective-permute-start.3
  472.8 2.2 collective-permute-start.3
  481.0 2.2 collective-permute-start.3
  489.2 2.2 collective-permute-start.3
  497.4 2.2 collective-permute-start.3
  505.5 2.2 collective-permute-start.3
  513.7 2.2 collective-permute-start.3
  521.9 2.2 collective-permute-start.3
  530.1 2.2 collective-permute-start.3
  (701 shorter events, 219.5 us)
Async XLA Ops:
  7.2 68.1 %all-gather.4.cloned.1.call-start = ((), (), s32[]{:S(2)}) async-start(), calls=%async_computation.1 | async-start | bytes 2359296 | tf_op jit(solution)/shard_map/all_gather | solution.py:37
  9.4 189.6 %all-gather.6.cloned.1.call-start = ((), (), s32[]{:S(2)}) async-start(), calls=%async_computation.2 | async-start | bytes 17301504 | tf_op jit(solution)/shard_map/all_gather | solution.py:40
  11.3 42.3 %all-to-all-start = ((bf16[32,128,128]{2,1,0:T(8,128)(2,1)}), bf16[32,128,128]{2,1,0:T(8,128)(2,1)S(1)}, u32[]{:S(2)}, u32[]{:S(2)}) async-start(bf16[32,128,128]{2,1,0:T(8,128)(2,1)} %stack.2), calls=%async_computation | async-start | bytes 2097152 | tf_op jit(solution)/shard_map/all_to_all | solution.py:77
  21.2 243.0 %all-gather.8.cloned.1.call-start = ((), (), s32[]{:S(2)}) async-start(), calls=%async_computation.3 | async-start | bytes 1081344 | tf_op jit(solution)/shard_map/all_gather | solution.py:79
  275.9 5.9 %collective-permute-start.2 = (f32[128,128]{1,0:T(8,128)S(1)}, f32[128,128]{1,0:T(8,128)S(1)}, u32[]{:S(2)}, u32[]{:S(2)}) collective-permute-start(f32[128,128]{1,0:T(8,128)S(1)} %fusion.89), channel_id=1, source_target_pairs={{0,8},{8,16},{16,24},{24,32},{32,40},{40,48},{48,56},{56,64},{64,7... | collective-permute-start | bytes 196616 | tf_op jit(solution)/shard_map/while/body/eval_jaxpr/ppermute | solution.py:14
  276.5 6.0 %collective-permute-start.3 = (f32[128,128]{1,0:T(8,128)S(1)}, f32[128,128]{1,0:T(8,128)S(1)}, u32[]{:S(2)}, u32[]{:S(2)}) collective-permute-start(f32[128,128]{1,0:T(8,128)S(1)} %fusion.90), channel_id=1, source_target_pairs={{0,8},{8,16},{16,24},{24,32},{32,40},{40,48},{48,56},{56,64},{64,7... | collective-permute-start | bytes 196616 | tf_op jit(solution)/shard_map/while/body/eval_jaxpr/ppermute | solution.py:14
  284.1 5.9 %collective-permute-start.2 = (f32[128,128]{1,0:T(8,128)S(1)}, f32[128,128]{1,0:T(8,128)S(1)}, u32[]{:S(2)}, u32[]{:S(2)}) collective-permute-start(f32[128,128]{1,0:T(8,128)S(1)} %fusion.89), channel_id=1, source_target_pairs={{0,8},{8,16},{16,24},{24,32},{32,40},{40,48},{48,56},{56,64},{64,7... | collective-permute-start | bytes 196616 | tf_op jit(solution)/shard_map/while/body/eval_jaxpr/ppermute | solution.py:14
  284.5 6.2 %collective-permute-start.3 = (f32[128,128]{1,0:T(8,128)S(1)}, f32[128,128]{1,0:T(8,128)S(1)}, u32[]{:S(2)}, u32[]{:S(2)}) collective-permute-start(f32[128,128]{1,0:T(8,128)S(1)} %fusion.90), channel_id=1, source_target_pairs={{0,8},{8,16},{16,24},{24,32},{32,40},{40,48},{48,56},{56,64},{64,7... | collective-permute-start | bytes 196616 | tf_op jit(solution)/shard_map/while/body/eval_jaxpr/ppermute | solution.py:14
  292.3 5.9 %collective-permute-start.2 = (f32[128,128]{1,0:T(8,128)S(1)}, f32[128,128]{1,0:T(8,128)S(1)}, u32[]{:S(2)}, u32[]{:S(2)}) collective-permute-start(f32[128,128]{1,0:T(8,128)S(1)} %fusion.89), channel_id=1, source_target_pairs={{0,8},{8,16},{16,24},{24,32},{32,40},{40,48},{48,56},{56,64},{64,7... | collective-permute-start | bytes 196616 | tf_op jit(solution)/shard_map/while/body/eval_jaxpr/ppermute | solution.py:14
  292.7 6.2 %collective-permute-start.3 = (f32[128,128]{1,0:T(8,128)S(1)}, f32[128,128]{1,0:T(8,128)S(1)}, u32[]{:S(2)}, u32[]{:S(2)}) collective-permute-start(f32[128,128]{1,0:T(8,128)S(1)} %fusion.90), channel_id=1, source_target_pairs={{0,8},{8,16},{16,24},{24,32},{32,40},{40,48},{48,56},{56,64},{64,7... | collective-permute-start | bytes 196616 | tf_op jit(solution)/shard_map/while/body/eval_jaxpr/ppermute | solution.py:14
  300.5 5.9 %collective-permute-start.2 = (f32[128,128]{1,0:T(8,128)S(1)}, f32[128,128]{1,0:T(8,128)S(1)}, u32[]{:S(2)}, u32[]{:S(2)}) collective-permute-start(f32[128,128]{1,0:T(8,128)S(1)} %fusion.89), channel_id=1, source_target_pairs={{0,8},{8,16},{16,24},{24,32},{32,40},{40,48},{48,56},{56,64},{64,7... | collective-permute-start | bytes 196616 | tf_op jit(solution)/shard_map/while/body/eval_jaxpr/ppermute | solution.py:14
  300.8 6.2 %collective-permute-start.3 = (f32[128,128]{1,0:T(8,128)S(1)}, f32[128,128]{1,0:T(8,128)S(1)}, u32[]{:S(2)}, u32[]{:S(2)}) collective-permute-start(f32[128,128]{1,0:T(8,128)S(1)} %fusion.90), channel_id=1, source_target_pairs={{0,8},{8,16},{16,24},{24,32},{32,40},{40,48},{48,56},{56,64},{64,7... | collective-permute-start | bytes 196616 | tf_op jit(solution)/shard_map/while/body/eval_jaxpr/ppermute | solution.py:14
  309.0 6.2 %collective-permute-start.3 = (f32[128,128]{1,0:T(8,128)S(1)}, f32[128,128]{1,0:T(8,128)S(1)}, u32[]{:S(2)}, u32[]{:S(2)}) collective-permute-start(f32[128,128]{1,0:T(8,128)S(1)} %fusion.90), channel_id=1, source_target_pairs={{0,8},{8,16},{16,24},{24,32},{32,40},{40,48},{48,56},{56,64},{64,7... | collective-permute-start | bytes 196616 | tf_op jit(solution)/shard_map/while/body/eval_jaxpr/ppermute | solution.py:14
  317.2 6.2 %collective-permute-start.3 = (f32[128,128]{1,0:T(8,128)S(1)}, f32[128,128]{1,0:T(8,128)S(1)}, u32[]{:S(2)}, u32[]{:S(2)}) collective-permute-start(f32[128,128]{1,0:T(8,128)S(1)} %fusion.90), channel_id=1, source_target_pairs={{0,8},{8,16},{16,24},{24,32},{32,40},{40,48},{48,56},{56,64},{64,7... | collective-permute-start | bytes 196616 | tf_op jit(solution)/shard_map/while/body/eval_jaxpr/ppermute | solution.py:14
  325.4 6.2 %collective-permute-start.3 = (f32[128,128]{1,0:T(8,128)S(1)}, f32[128,128]{1,0:T(8,128)S(1)}, u32[]{:S(2)}, u32[]{:S(2)}) collective-permute-start(f32[128,128]{1,0:T(8,128)S(1)} %fusion.90), channel_id=1, source_target_pairs={{0,8},{8,16},{16,24},{24,32},{32,40},{40,48},{48,56},{56,64},{64,7... | collective-permute-start | bytes 196616 | tf_op jit(solution)/shard_map/while/body/eval_jaxpr/ppermute | solution.py:14
  333.2 5.9 %collective-permute-start.2 = (f32[128,128]{1,0:T(8,128)S(1)}, f32[128,128]{1,0:T(8,128)S(1)}, u32[]{:S(2)}, u32[]{:S(2)}) collective-permute-start(f32[128,128]{1,0:T(8,128)S(1)} %fusion.89), channel_id=1, source_target_pairs={{0,8},{8,16},{16,24},{24,32},{32,40},{40,48},{48,56},{56,64},{64,7... | collective-permute-start | bytes 196616 | tf_op jit(solution)/shard_map/while/body/eval_jaxpr/ppermute | solution.py:14
  333.5 6.2 %collective-permute-start.3 = (f32[128,128]{1,0:T(8,128)S(1)}, f32[128,128]{1,0:T(8,128)S(1)}, u32[]{:S(2)}, u32[]{:S(2)}) collective-permute-start(f32[128,128]{1,0:T(8,128)S(1)} %fusion.90), channel_id=1, source_target_pairs={{0,8},{8,16},{16,24},{24,32},{32,40},{40,48},{48,56},{56,64},{64,7... | collective-permute-start | bytes 196616 | tf_op jit(solution)/shard_map/while/body/eval_jaxpr/ppermute | solution.py:14
  342.0 6.1 %collective-permute-start.3 = (f32[128,128]{1,0:T(8,128)S(1)}, f32[128,128]{1,0:T(8,128)S(1)}, u32[]{:S(2)}, u32[]{:S(2)}) collective-permute-start(f32[128,128]{1,0:T(8,128)S(1)} %fusion.90), channel_id=1, source_target_pairs={{0,8},{8,16},{16,24},{24,32},{32,40},{40,48},{48,56},{56,64},{64,7... | collective-permute-start | bytes 196616 | tf_op jit(solution)/shard_map/while/body/eval_jaxpr/ppermute | solution.py:14
  349.7 5.9 %collective-permute-start.2 = (f32[128,128]{1,0:T(8,128)S(1)}, f32[128,128]{1,0:T(8,128)S(1)}, u32[]{:S(2)}, u32[]{:S(2)}) collective-permute-start(f32[128,128]{1,0:T(8,128)S(1)} %fusion.89), channel_id=1, source_target_pairs={{0,8},{8,16},{16,24},{24,32},{32,40},{40,48},{48,56},{56,64},{64,7... | collective-permute-start | bytes 196616 | tf_op jit(solution)/shard_map/while/body/eval_jaxpr/ppermute | solution.py:14
  350.2 6.1 %collective-permute-start.3 = (f32[128,128]{1,0:T(8,128)S(1)}, f32[128,128]{1,0:T(8,128)S(1)}, u32[]{:S(2)}, u32[]{:S(2)}) collective-permute-start(f32[128,128]{1,0:T(8,128)S(1)} %fusion.90), channel_id=1, source_target_pairs={{0,8},{8,16},{16,24},{24,32},{32,40},{40,48},{48,56},{56,64},{64,7... | collective-permute-start | bytes 196616 | tf_op jit(solution)/shard_map/while/body/eval_jaxpr/ppermute | solution.py:14
  357.9 5.9 %collective-permute-start.2 = (f32[128,128]{1,0:T(8,128)S(1)}, f32[128,128]{1,0:T(8,128)S(1)}, u32[]{:S(2)}, u32[]{:S(2)}) collective-permute-start(f32[128,128]{1,0:T(8,128)S(1)} %fusion.89), channel_id=1, source_target_pairs={{0,8},{8,16},{16,24},{24,32},{32,40},{40,48},{48,56},{56,64},{64,7... | collective-permute-start | bytes 196616 | tf_op jit(solution)/shard_map/while/body/eval_jaxpr/ppermute | solution.py:14
  358.3 6.1 %collective-permute-start.3 = (f32[128,128]{1,0:T(8,128)S(1)}, f32[128,128]{1,0:T(8,128)S(1)}, u32[]{:S(2)}, u32[]{:S(2)}) collective-permute-start(f32[128,128]{1,0:T(8,128)S(1)} %fusion.90), channel_id=1, source_target_pairs={{0,8},{8,16},{16,24},{24,32},{32,40},{40,48},{48,56},{56,64},{64,7... | collective-permute-start | bytes 196616 | tf_op jit(solution)/shard_map/while/body/eval_jaxpr/ppermute | solution.py:14
  366.1 5.9 %collective-permute-start.2 = (f32[128,128]{1,0:T(8,128)S(1)}, f32[128,128]{1,0:T(8,128)S(1)}, u32[]{:S(2)}, u32[]{:S(2)}) collective-permute-start(f32[128,128]{1,0:T(8,128)S(1)} %fusion.89), channel_id=1, source_target_pairs={{0,8},{8,16},{16,24},{24,32},{32,40},{40,48},{48,56},{56,64},{64,7... | collective-permute-start | bytes 196616 | tf_op jit(solution)/shard_map/while/body/eval_jaxpr/ppermute | solution.py:14
  366.5 6.1 %collective-permute-start.3 = (f32[128,128]{1,0:T(8,128)S(1)}, f32[128,128]{1,0:T(8,128)S(1)}, u32[]{:S(2)}, u32[]{:S(2)}) collective-permute-start(f32[128,128]{1,0:T(8,128)S(1)} %fusion.90), channel_id=1, source_target_pairs={{0,8},{8,16},{16,24},{24,32},{32,40},{40,48},{48,56},{56,64},{64,7... | collective-permute-start | bytes 196616 | tf_op jit(solution)/shard_map/while/body/eval_jaxpr/ppermute | solution.py:14
  374.3 5.9 %collective-permute-start.2 = (f32[128,128]{1,0:T(8,128)S(1)}, f32[128,128]{1,0:T(8,128)S(1)}, u32[]{:S(2)}, u32[]{:S(2)}) collective-permute-start(f32[128,128]{1,0:T(8,128)S(1)} %fusion.89), channel_id=1, source_target_pairs={{0,8},{8,16},{16,24},{24,32},{32,40},{40,48},{48,56},{56,64},{64,7... | collective-permute-start | bytes 196616 | tf_op jit(solution)/shard_map/while/body/eval_jaxpr/ppermute | solution.py:14
  374.7 6.1 %collective-permute-start.3 = (f32[128,128]{1,0:T(8,128)S(1)}, f32[128,128]{1,0:T(8,128)S(1)}, u32[]{:S(2)}, u32[]{:S(2)}) collective-permute-start(f32[128,128]{1,0:T(8,128)S(1)} %fusion.90), channel_id=1, source_target_pairs={{0,8},{8,16},{16,24},{24,32},{32,40},{40,48},{48,56},{56,64},{64,7... | collective-permute-start | bytes 196616 | tf_op jit(solution)/shard_map/while/body/eval_jaxpr/ppermute | solution.py:14
  382.4 5.9 %collective-permute-start.2 = (f32[128,128]{1,0:T(8,128)S(1)}, f32[128,128]{1,0:T(8,128)S(1)}, u32[]{:S(2)}, u32[]{:S(2)}) collective-permute-start(f32[128,128]{1,0:T(8,128)S(1)} %fusion.89), channel_id=1, source_target_pairs={{0,8},{8,16},{16,24},{24,32},{32,40},{40,48},{48,56},{56,64},{64,7... | collective-permute-start | bytes 196616 | tf_op jit(solution)/shard_map/while/body/eval_jaxpr/ppermute | solution.py:14
  382.9 6.1 %collective-permute-start.3 = (f32[128,128]{1,0:T(8,128)S(1)}, f32[128,128]{1,0:T(8,128)S(1)}, u32[]{:S(2)}, u32[]{:S(2)}) collective-permute-start(f32[128,128]{1,0:T(8,128)S(1)} %fusion.90), channel_id=1, source_target_pairs={{0,8},{8,16},{16,24},{24,32},{32,40},{40,48},{48,56},{56,64},{64,7... | collective-permute-start | bytes 196616 | tf_op jit(solution)/shard_map/while/body/eval_jaxpr/ppermute | solution.py:14
  391.0 6.1 %collective-permute-start.3 = (f32[128,128]{1,0:T(8,128)S(1)}, f32[128,128]{1,0:T(8,128)S(1)}, u32[]{:S(2)}, u32[]{:S(2)}) collective-permute-start(f32[128,128]{1,0:T(8,128)S(1)} %fusion.90), channel_id=1, source_target_pairs={{0,8},{8,16},{16,24},{24,32},{32,40},{40,48},{48,56},{56,64},{64,7... | collective-permute-start | bytes 196616 | tf_op jit(solution)/shard_map/while/body/eval_jaxpr/ppermute | solution.py:14
  398.8 5.9 %collective-permute-start.2 = (f32[128,128]{1,0:T(8,128)S(1)}, f32[128,128]{1,0:T(8,128)S(1)}, u32[]{:S(2)}, u32[]{:S(2)}) collective-permute-start(f32[128,128]{1,0:T(8,128)S(1)} %fusion.89), channel_id=1, source_target_pairs={{0,8},{8,16},{16,24},{24,32},{32,40},{40,48},{48,56},{56,64},{64,7... | collective-permute-start | bytes 196616 | tf_op jit(solution)/shard_map/while/body/eval_jaxpr/ppermute | solution.py:14
  399.2 6.1 %collective-permute-start.3 = (f32[128,128]{1,0:T(8,128)S(1)}, f32[128,128]{1,0:T(8,128)S(1)}, u32[]{:S(2)}, u32[]{:S(2)}) collective-permute-start(f32[128,128]{1,0:T(8,128)S(1)} %fusion.90), channel_id=1, source_target_pairs={{0,8},{8,16},{16,24},{24,32},{32,40},{40,48},{48,56},{56,64},{64,7... | collective-permute-start | bytes 196616 | tf_op jit(solution)/shard_map/while/body/eval_jaxpr/ppermute | solution.py:14
  407.0 5.9 %collective-permute-start.2 = (f32[128,128]{1,0:T(8,128)S(1)}, f32[128,128]{1,0:T(8,128)S(1)}, u32[]{:S(2)}, u32[]{:S(2)}) collective-permute-start(f32[128,128]{1,0:T(8,128)S(1)} %fusion.89), channel_id=1, source_target_pairs={{0,8},{8,16},{16,24},{24,32},{32,40},{40,48},{48,56},{56,64},{64,7... | collective-permute-start | bytes 196616 | tf_op jit(solution)/shard_map/while/body/eval_jaxpr/ppermute | solution.py:14
  407.4 6.1 %collective-permute-start.3 = (f32[128,128]{1,0:T(8,128)S(1)}, f32[128,128]{1,0:T(8,128)S(1)}, u32[]{:S(2)}, u32[]{:S(2)}) collective-permute-start(f32[128,128]{1,0:T(8,128)S(1)} %fusion.90), channel_id=1, source_target_pairs={{0,8},{8,16},{16,24},{24,32},{32,40},{40,48},{48,56},{56,64},{64,7... | collective-permute-start | bytes 196616 | tf_op jit(solution)/shard_map/while/body/eval_jaxpr/ppermute | solution.py:14
  415.6 6.1 %collective-permute-start.3 = (f32[128,128]{1,0:T(8,128)S(1)}, f32[128,128]{1,0:T(8,128)S(1)}, u32[]{:S(2)}, u32[]{:S(2)}) collective-permute-start(f32[128,128]{1,0:T(8,128)S(1)} %fusion.90), channel_id=1, source_target_pairs={{0,8},{8,16},{16,24},{24,32},{32,40},{40,48},{48,56},{56,64},{64,7... | collective-permute-start | bytes 196616 | tf_op jit(solution)/shard_map/while/body/eval_jaxpr/ppermute | solution.py:14
  423.8 6.1 %collective-permute-start.3 = (f32[128,128]{1,0:T(8,128)S(1)}, f32[128,128]{1,0:T(8,128)S(1)}, u32[]{:S(2)}, u32[]{:S(2)}) collective-permute-start(f32[128,128]{1,0:T(8,128)S(1)} %fusion.90), channel_id=1, source_target_pairs={{0,8},{8,16},{16,24},{24,32},{32,40},{40,48},{48,56},{56,64},{64,7... | collective-permute-start | bytes 196616 | tf_op jit(solution)/shard_map/while/body/eval_jaxpr/ppermute | solution.py:14
  431.9 6.1 %collective-permute-start.3 = (f32[128,128]{1,0:T(8,128)S(1)}, f32[128,128]{1,0:T(8,128)S(1)}, u32[]{:S(2)}, u32[]{:S(2)}) collective-permute-start(f32[128,128]{1,0:T(8,128)S(1)} %fusion.90), channel_id=1, source_target_pairs={{0,8},{8,16},{16,24},{24,32},{32,40},{40,48},{48,56},{56,64},{64,7... | collective-permute-start | bytes 196616 | tf_op jit(solution)/shard_map/while/body/eval_jaxpr/ppermute | solution.py:14
  440.1 6.1 %collective-permute-start.3 = (f32[128,128]{1,0:T(8,128)S(1)}, f32[128,128]{1,0:T(8,128)S(1)}, u32[]{:S(2)}, u32[]{:S(2)}) collective-permute-start(f32[128,128]{1,0:T(8,128)S(1)} %fusion.90), channel_id=1, source_target_pairs={{0,8},{8,16},{16,24},{24,32},{32,40},{40,48},{48,56},{56,64},{64,7... | collective-permute-start | bytes 196616 | tf_op jit(solution)/shard_map/while/body/eval_jaxpr/ppermute | solution.py:14
  448.3 6.1 %collective-permute-start.3 = (f32[128,128]{1,0:T(8,128)S(1)}, f32[128,128]{1,0:T(8,128)S(1)}, u32[]{:S(2)}, u32[]{:S(2)}) collective-permute-start(f32[128,128]{1,0:T(8,128)S(1)} %fusion.90), channel_id=1, source_target_pairs={{0,8},{8,16},{16,24},{24,32},{32,40},{40,48},{48,56},{56,64},{64,7... | collective-permute-start | bytes 196616 | tf_op jit(solution)/shard_map/while/body/eval_jaxpr/ppermute | solution.py:14
  456.5 6.1 %collective-permute-start.3 = (f32[128,128]{1,0:T(8,128)S(1)}, f32[128,128]{1,0:T(8,128)S(1)}, u32[]{:S(2)}, u32[]{:S(2)}) collective-permute-start(f32[128,128]{1,0:T(8,128)S(1)} %fusion.90), channel_id=1, source_target_pairs={{0,8},{8,16},{16,24},{24,32},{32,40},{40,48},{48,56},{56,64},{64,7... | collective-permute-start | bytes 196616 | tf_op jit(solution)/shard_map/while/body/eval_jaxpr/ppermute | solution.py:14
  464.6 6.1 %collective-permute-start.3 = (f32[128,128]{1,0:T(8,128)S(1)}, f32[128,128]{1,0:T(8,128)S(1)}, u32[]{:S(2)}, u32[]{:S(2)}) collective-permute-start(f32[128,128]{1,0:T(8,128)S(1)} %fusion.90), channel_id=1, source_target_pairs={{0,8},{8,16},{16,24},{24,32},{32,40},{40,48},{48,56},{56,64},{64,7... | collective-permute-start | bytes 196616 | tf_op jit(solution)/shard_map/while/body/eval_jaxpr/ppermute | solution.py:14
  472.8 6.1 %collective-permute-start.3 = (f32[128,128]{1,0:T(8,128)S(1)}, f32[128,128]{1,0:T(8,128)S(1)}, u32[]{:S(2)}, u32[]{:S(2)}) collective-permute-start(f32[128,128]{1,0:T(8,128)S(1)} %fusion.90), channel_id=1, source_target_pairs={{0,8},{8,16},{16,24},{24,32},{32,40},{40,48},{48,56},{56,64},{64,7... | collective-permute-start | bytes 196616 | tf_op jit(solution)/shard_map/while/body/eval_jaxpr/ppermute | solution.py:14
  481.0 6.1 %collective-permute-start.3 = (f32[128,128]{1,0:T(8,128)S(1)}, f32[128,128]{1,0:T(8,128)S(1)}, u32[]{:S(2)}, u32[]{:S(2)}) collective-permute-start(f32[128,128]{1,0:T(8,128)S(1)} %fusion.90), channel_id=1, source_target_pairs={{0,8},{8,16},{16,24},{24,32},{32,40},{40,48},{48,56},{56,64},{64,7... | collective-permute-start | bytes 196616 | tf_op jit(solution)/shard_map/while/body/eval_jaxpr/ppermute | solution.py:14
  489.2 6.1 %collective-permute-start.3 = (f32[128,128]{1,0:T(8,128)S(1)}, f32[128,128]{1,0:T(8,128)S(1)}, u32[]{:S(2)}, u32[]{:S(2)}) collective-permute-start(f32[128,128]{1,0:T(8,128)S(1)} %fusion.90), channel_id=1, source_target_pairs={{0,8},{8,16},{16,24},{24,32},{32,40},{40,48},{48,56},{56,64},{64,7... | collective-permute-start | bytes 196616 | tf_op jit(solution)/shard_map/while/body/eval_jaxpr/ppermute | solution.py:14
  497.4 6.1 %collective-permute-start.3 = (f32[128,128]{1,0:T(8,128)S(1)}, f32[128,128]{1,0:T(8,128)S(1)}, u32[]{:S(2)}, u32[]{:S(2)}) collective-permute-start(f32[128,128]{1,0:T(8,128)S(1)} %fusion.90), channel_id=1, source_target_pairs={{0,8},{8,16},{16,24},{24,32},{32,40},{40,48},{48,56},{56,64},{64,7... | collective-permute-start | bytes 196616 | tf_op jit(solution)/shard_map/while/body/eval_jaxpr/ppermute | solution.py:14
  505.5 6.1 %collective-permute-start.3 = (f32[128,128]{1,0:T(8,128)S(1)}, f32[128,128]{1,0:T(8,128)S(1)}, u32[]{:S(2)}, u32[]{:S(2)}) collective-permute-start(f32[128,128]{1,0:T(8,128)S(1)} %fusion.90), channel_id=1, source_target_pairs={{0,8},{8,16},{16,24},{24,32},{32,40},{40,48},{48,56},{56,64},{64,7... | collective-permute-start | bytes 196616 | tf_op jit(solution)/shard_map/while/body/eval_jaxpr/ppermute | solution.py:14
  513.7 6.1 %collective-permute-start.3 = (f32[128,128]{1,0:T(8,128)S(1)}, f32[128,128]{1,0:T(8,128)S(1)}, u32[]{:S(2)}, u32[]{:S(2)}) collective-permute-start(f32[128,128]{1,0:T(8,128)S(1)} %fusion.90), channel_id=1, source_target_pairs={{0,8},{8,16},{16,24},{24,32},{32,40},{40,48},{48,56},{56,64},{64,7... | collective-permute-start | bytes 196616 | tf_op jit(solution)/shard_map/while/body/eval_jaxpr/ppermute | solution.py:14
  521.9 6.1 %collective-permute-start.3 = (f32[128,128]{1,0:T(8,128)S(1)}, f32[128,128]{1,0:T(8,128)S(1)}, u32[]{:S(2)}, u32[]{:S(2)}) collective-permute-start(f32[128,128]{1,0:T(8,128)S(1)} %fusion.90), channel_id=1, source_target_pairs={{0,8},{8,16},{16,24},{24,32},{32,40},{40,48},{48,56},{56,64},{64,7... | collective-permute-start | bytes 196616 | tf_op jit(solution)/shard_map/while/body/eval_jaxpr/ppermute | solution.py:14
  530.1 6.1 %collective-permute-start.3 = (f32[128,128]{1,0:T(8,128)S(1)}, f32[128,128]{1,0:T(8,128)S(1)}, u32[]{:S(2)}, u32[]{:S(2)}) collective-permute-start(f32[128,128]{1,0:T(8,128)S(1)} %fusion.90), channel_id=1, source_target_pairs={{0,8},{8,16},{16,24},{24,32},{32,40},{40,48},{48,56},{56,64},{64,7... | collective-permute-start | bytes 196616 | tf_op jit(solution)/shard_map/while/body/eval_jaxpr/ppermute | solution.py:14
  (86 other events, 544.9 us)
Sparse Core Ops, SparseCore 0:
  10.6 64.6 all-gather.3
  77.0 121.9 all-gather.5
  201.4 62.7 all-gather.7
